TPU v7x, 512 devices: a whole 4x4x16 slice. The times are simulated.
512 devices in a mesh: ctx: 64 (over y_hi, z, core), dp: 8 (over x, y_lo).
Axes of the slice: x: 4, y: 4 (y_hi: 2, y_lo: 2; y = y_hi * 2 + y_lo), z: 16, core: 2. Of those that a mesh axis runs over, the one named last changes fastest.
Arguments:
- queries: bfloat16 [8192, 2048], P('ctx', 'dp')
- keys: bfloat16 [8192, 2048], P('ctx', 'dp')
- values: bfloat16 [8192, 2048], P('ctx', 'dp'), may hold values from -6 to 6
- old_keys: bfloat16 [2048, 2048], P('ctx', 'dp'), may hold values from -6 to 6
- old_values: bfloat16 [2048, 2048], P('ctx', 'dp'), may hold values from -6 to 6
- conv_keys: bfloat16 [16, 4, 128, 128], P('dp'), may hold values from -0.25 to 0.25
- conv_values: bfloat16 [16, 4, 128, 128], P('dp'), may hold values from -0.25 to 0.25
- out_proj: bfloat16 [4096, 2048], P('ctx', 'dp'), may hold values from -0.125 to 0.125
- residual: bfloat16 [8192, 4096], P('ctx', 'dp'), may hold values from -4 to 4
- gain: bfloat16 [4096], P('dp'), may hold values from 0.5 to 1.5
- span_order: int32 [128], P('ctx'), may hold values from 0 to 127, as said below
- memory_length: int32 [1], replicated, may hold values from 128 to 512
Outputs:
- layer_out: bfloat16 [8192, 4096], P('ctx', 'dp')
Inputs may be any that keep to these rules, and one draw needn't show every extreme that they name: `span_order`: entries 2 i and 2 i + 1 are blocks c and 127 - c for some c, in either order; every block appears once. `memory_length`: the valid slots are the last ones.
All inputs are finite; a program needn't handle non-finite values.
Results may differ from a plain program's by a relative error of at most 0.018.
Values may be sent and summed in bfloat16 or wider, within the bound.
A program may use at most 64 MiB of HBM per device.

v0:
```python
import math

import jax
import jax.numpy as jnp
from jax import lax
from jax.sharding import PartitionSpec as P

neg_big = -1e30


def compress(old, conv_weight):
    slots = old.shape[0] // 4
    groups = conv_weight.shape[0]
    width = conv_weight.shape[2]
    grouped = old.reshape(slots, 4, groups, width)
    mixed = jnp.einsum("jthc,htce->jhe", grouped, conv_weight, preferred_element_type=jnp.float32)
    return mixed.reshape(slots, groups * width).astype(jnp.bfloat16)


def attend(carry, queries3, key_rows, value_rows, allowed, scale):
    run_max, run_sum, run_acc = carry
    rows = key_rows.shape[0]
    groups = queries3.shape[1]
    width = queries3.shape[2]
    keys3 = key_rows.reshape(rows, groups, width)
    values3 = value_rows.reshape(rows, groups, width)
    scores = jnp.einsum("thd,rhd->htr", queries3, keys3, preferred_element_type=jnp.float32) * scale
    scores = jnp.where(allowed[None], scores, neg_big)
    new_max = jnp.maximum(run_max, jnp.max(scores, axis=2))
    weights = jnp.where(allowed[None], jnp.exp(scores - new_max[:, :, None]), 0.0)
    factor = jnp.exp(run_max - new_max)
    new_sum = run_sum * factor + jnp.sum(weights, axis=2)
    update = jnp.einsum(
        "htr,rhd->htd", weights.astype(jnp.bfloat16), values3, preferred_element_type=jnp.float32
    )
    return (new_max, new_sum, run_acc * factor[:, :, None] + update)


def local(
    queries,
    keys,
    values,
    old_keys,
    old_values,
    conv_keys,
    conv_values,
    out_proj,
    residual,
    gain,
    span_order,
    memory_length,
):
    tok_rows = queries.shape[0]
    groups = conv_keys.shape[0]
    width = conv_keys.shape[2]
    half_rows = tok_rows // 2
    scale = 1.0 / math.sqrt(width)
    ctx_count = lax.axis_size("ctx")
    gain_f = gain.astype(jnp.float32)[None, :]
    offsets = jnp.arange(half_rows, dtype=jnp.int32)
    query_pos = (span_order[:, None] * half_rows + offsets[None, :]).reshape(tok_rows)
    queries3 = queries.reshape(tok_rows, groups, width)
    table = lax.all_gather(span_order, "ctx", axis=0, tiled=True)
    slot_count = old_keys.shape[0] // 4 * ctx_count
    first_valid = slot_count - memory_length[0]
    start_carry = (
        jnp.full((groups, tok_rows), neg_big, jnp.float32),
        jnp.zeros((groups, tok_rows), jnp.float32),
        jnp.zeros((groups, tok_rows, width), jnp.float32),
    )
    whole_keys, whole_values = (
        lax.all_gather(old_keys, "ctx", axis=0, tiled=True),
        lax.all_gather(old_values, "ctx", axis=0, tiled=True),
    )
    mem_keys = compress(whole_keys, conv_keys)
    mem_values = compress(whole_values, conv_values)
    slot_index = jnp.arange(slot_count, dtype=jnp.int32)
    visible = jnp.broadcast_to((slot_index >= first_valid)[None, :], (tok_rows, slot_count))
    carry = attend(start_carry, queries3, mem_keys, mem_values, visible, scale)
    span_ids = jnp.arange(table.shape[0], dtype=jnp.int32)
    pieces = (
        lax.all_gather(keys, "ctx", axis=0, tiled=True),
        lax.all_gather(values, "ctx", axis=0, tiled=True),
    )
    rows = pieces[0].shape[0]
    index = jnp.arange(rows, dtype=jnp.int32)
    slot_span = index // half_rows
    picked = jnp.sum(jnp.where(slot_span[:, None] == span_ids[None, :], table[None, :], 0), axis=1)
    key_pos = picked * half_rows + index % half_rows
    visible = key_pos[None, :] <= query_pos[:, None]
    run_max, run_sum, run_acc = attend(carry, queries3, pieces[0], pieces[1], visible, scale)
    attn = (
        (run_acc / run_sum[:, :, None])
        .transpose(1, 0, 2)
        .reshape(tok_rows, groups * width)
        .astype(jnp.bfloat16)
    )
    partial_sums = lax.dot_general(
        attn,
        lax.all_gather(out_proj, "ctx", axis=0, tiled=True),
        (((1,), (1,)), ((), ())),
        preferred_element_type=jnp.float32,
    )
    features = partial_sums.shape[1]
    share = lax.psum_scatter(
        partial_sums.astype(jnp.bfloat16), "dp", scatter_dimension=1, tiled=True
    ).astype(jnp.float32)
    stream = residual.astype(jnp.float32) + share
    power = lax.psum(jnp.sum(stream * stream, axis=1), "dp") / features
    normed = stream * lax.rsqrt(power + 1e-06)[:, None] * gain_f
    return normed.astype(jnp.bfloat16)


def solution(mesh):
    placed = (
        P("ctx", "dp"),
        P("ctx", "dp"),
        P("ctx", "dp"),
        P("ctx", "dp"),
        P("ctx", "dp"),
        P("dp", None, None, None),
        P("dp", None, None, None),
        P("ctx", "dp"),
        P("ctx", "dp"),
        P("dp"),
        P("ctx"),
        P(),
    )
    return jax.shard_map(
        local, mesh=mesh, in_specs=placed, out_specs=P("ctx", "dp"), check_vma=False
    )
```

profile of v0, /device:TPU:1, one launch (start us, length us, event | category | flops | bytes accessed | tf_op | source)
XLA Modules:
  0.0 796.7 jit_solution(13249138557412104678)
XLA Ops:
  6.5 0.7 all-gather.6.cloned.1.call-update
  7.3 0.7 all-gather.8.cloned.1.call-update
  8.1 0.7 all-gather.12.cloned.1.call-update
  8.8 1.6 copy.39
  10.4 0.5 all-gather.14.cloned.1.call-update
  11.0 0.7 broadcast_multiply_fusion
  11.7 1.3 dynamic-slice
  13.6 0.9 dynamic-update-slice
  14.5 28.4 %all-reduce = s32[128]{0:T(128)S(1)} all-reduce(s32[128]{0:T(128)S(1)} %dynamic-update-slice), channel_id=1, replica_groups=mesh['ctx'=64,'dp'=8] {'ctx'}, use_global_device_ids=true, to_apply=%add | all-reduce | flops 128 | bytes 1024
  42.9 2.5 select_reduce_fusion
  45.4 0.1 iota_add_fusion
  45.5 0.1 add.85
  45.6 0.6 broadcast_compare_fusion
  46.9 110.5 %all-gather.6.cloned.1.call-done = bf16[2048,256]{1,0:T(8,128)(2,1)} async-done(((bf16[32,256]{1,0:T(8,128)(2,1)}), bf16[2048,256]{1,0:T(8,128)(2,1)}) %all-gather.6.cloned.1.call-update) | async-done | bytes 1048592 | tf_op jit(solution)/shard_map/all_gather | solution.py:72
  157.4 1.3 reshape.125
  158.8 138.6 %all-gather.8.cloned.1.call-done = bf16[2048,256]{1,0:T(8,128)(2,1)} async-done(((bf16[32,256]{1,0:T(8,128)(2,1)}), bf16[2048,256]{1,0:T(8,128)(2,1)}) %all-gather.8.cloned.1.call-update) | async-done | bytes 1048592 | tf_op jit(solution)/shard_map/all_gather | solution.py:73
  297.4 1.3 reshape.127
  298.8 1.6 fusion.54
  300.3 146.9 %all-gather.12.cloned.1.call-done = bf16[8192,256]{1,0:T(8,128)(2,1)} async-done(((bf16[128,256]{1,0:T(8,128)(2,1)}), bf16[8192,256]{1,0:T(8,128)(2,1)}) %all-gather.12.cloned.1.call-update) | async-done | bytes 4194320 | tf_op jit(solution)/shard_map/all_gather | solution.py:83
  447.2 6.4 copy.42
  453.7 138.0 %all-gather.10.cloned.1.call-done = bf16[8192,256]{0,1:T(8,128)(2,1)} async-done(((bf16[128,256]{0,1:T(8,128)(2,1)}), bf16[8192,256]{0,1:T(8,128)(2,1)}) %all-gather.10.cloned.1.call-update) | async-done | bytes 4194320 | tf_op jit(solution)/shard_map/all_gather | solution.py:82
  591.7 4.6 fusion.57
  596.4 0.2 fusion.28
  596.5 2.1 fusion.1
  598.7 1.8 fusion.15
  600.5 0.6 fusion.23
  601.2 131.4 %all-gather.14.cloned.1.call-done = bf16[4096,256]{1,0:T(8,128)(2,1)} async-done(((bf16[64,256]{1,0:T(8,128)(2,1)}), bf16[4096,256]{1,0:T(8,128)(2,1)}) %all-gather.14.cloned.1.call-update) | async-done | bytes 2097168 | tf_op jit(solution)/shard_map/all_gather | solution.py:100
  732.6 3.4 convolution_convert_fusion
  736.0 37.0 %reduce-scatter.2.cloned.1.call-done = bf16[128,512]{1,0:T(8,128)(2,1)} async-done(((bf16[128,4096]{1,0:T(8,128)(2,1)}), bf16[128,512]{1,0:T(8,128)(2,1)}) %reduce-scatter.2.cloned.1.call-update) | async-done | bytes 131088 | tf_op jit(solution)/shard_map/reduce_scatter | solution.py:105
  773.1 1.0 multiply_reduce_fusion
  774.1 14.2 %psum.7 = f32[128]{0:T(128)S(1)} all-reduce(f32[128]{0:T(128)S(1)} %multiply_reduce_fusion), channel_id=1, replica_groups=mesh['ctx'=64,'dp'=8] {'dp'}, use_global_device_ids=true, to_apply=%region_7.8 | all-reduce | flops 128 | bytes 1024 | tf_op jit(solution)/shard_map/psum | solution.py:109
  788.2 1.7 multiply_convert_fusion
  (30 shorter events, 0.3 us)
Async XLA Ops:
  6.5 292.2 %copy-start = (bf16[2,4,128,128]{3,2,1,0:T(8,128)(2,1)S(1)}, bf16[2,4,128,128]{3,2,1,0:T(8,128)(2,1)}, u32[]{:S(2)}) copy-start(bf16[2,4,128,128]{3,2,1,0:T(8,128)(2,1)} %param.17) | copy-start | bytes 786436
  6.5 292.2 %copy-start.4 = (bf16[128,256]{1,0:T(8,128)(2,1)S(1)}, bf16[128,256]{1,0:T(8,128)(2,1)}, u32[]{:S(2)}) copy-start(bf16[128,256]{1,0:T(8,128)(2,1)} %param.12) | copy-start | bytes 196612
  6.5 150.9 %all-gather.6.cloned.1.call-start = ((), (), s32[]{:S(2)}) async-start(), calls=%async_computation.1 | async-start | bytes 1064960 | tf_op jit(solution)/shard_map/all_gather | solution.py:72
  7.3 290.1 %all-gather.8.cloned.1.call-start = ((), (), s32[]{:S(2)}) async-start(), calls=%async_computation.2 | async-start | bytes 1064960 | tf_op jit(solution)/shard_map/all_gather | solution.py:73
  8.0 439.2 %all-gather.12.cloned.1.call-start = ((), (), s32[]{:S(2)}) async-start(), calls=%async_computation.4 | async-start | bytes 4259840 | tf_op jit(solution)/shard_map/all_gather | solution.py:83
  8.7 582.9 %all-gather.10.cloned.1.call-start = ((), (), s32[]{:S(2)}) async-start(), calls=%async_computation.3 | async-start | bytes 4259840 | tf_op jit(solution)/shard_map/all_gather | solution.py:82
  10.4 722.2 %all-gather.14.cloned.1.call-start = ((), (), s32[]{:S(2)}) async-start(), calls=%async_computation.5 | async-start | bytes 2129920 | tf_op jit(solution)/shard_map/all_gather | solution.py:100
  11.0 762.1 %reduce-scatter.2.cloned.1.call-start = ((), (), s32[]{:S(2)}) async-start(), calls=%async_computation.6 | async-start | bytes 1179648 | tf_op jit(solution)/shard_map/reduce_scatter | solution.py:105
  591.7 4.7 copy-start.2
  596.5 2.2 copy-start.1
  598.7 1.8 copy-start.6
  600.5 135.5 %copy-start.5 = (bf16[512]{0:T(512)(128)(2,1)S(1)}, bf16[512]{0:T(512)(128)(2,1)}, u32[]{:S(2)}) copy-start(bf16[512]{0:T(512)(128)(2,1)} %param.21) | copy-start | bytes 3076
  600.5 172.5 %copy-start.3 = (bf16[128,512]{1,0:T(8,128)(2,1)S(1)}, bf16[128,512]{1,0:T(8,128)(2,1)}, u32[]{:S(2)}) copy-start(bf16[128,512]{1,0:T(8,128)(2,1)} %param.20) | copy-start | bytes 393220
Sparse Core Ops, SparseCore 0:
  10.6 146.7 all-gather.5
  160.7 136.6 all-gather.7
  300.7 146.4 all-gather.11
  450.1 141.5 all-gather.9
  594.8 137.7 all-gather.13
  736.1 36.8 reduce-scatter.1
where the time goes:
time: 804 us; the launch traced here: 797 us
  waiting for transfers between devices  705 us (88%)
  blocking collectives  42.5 us (5%)
  between operations  14.9 us (2%)
  local copies, waits for them, and re-layouts  13 us (2%)
  matrix products  12 us (1%)
  other arithmetic  8.95 us (1%)
    all_gather x1, waiting for transfers between devices, local(): lax.all_gather(values, 'ctx', axis=0, tiled=True)  147 us
    all_gather x1, waiting for transfers between devices, local(): lax.all_gather(old_values, 'ctx', axis=0, tiled=True)  139 us
    all_gather x1, waiting for transfers between devices, local(): lax.all_gather(keys, 'ctx', axis=0, tiled=True)  138 us
    all_gather x1, waiting for transfers between devices, local(): lax.all_gather(out_proj, 'ctx', axis=0, tiled=True)  131 us
    all_gather x1, waiting for transfers between devices, local(): lax.all_gather(old_keys, 'ctx', axis=0, tiled=True)  111 us
    reduce_scatter x1, waiting for transfers between devices, local(): lax.psum_scatter(partial_sums.astype(jnp.bfloat16), 'dp', scatter_dimensi...  37 us
    unnamed x1, blocking collectives  28.4 us
  transfers between devices with their start and end apart: 6, of which 6 were waited for; matrix products, arithmetic and copies ran while one was open for 3% of the time, Pallas kernels for 0%

commit v1 on v0

v1 whole, which is shorter than its diff:
```python
import math

import jax
import jax.numpy as jnp
from jax import lax
from jax.experimental import pallas as pl
from jax.experimental.pallas import tpu as pltpu
from jax.sharding import PartitionSpec as P

MESH = pl.DeviceIdType.MESH
NEG = -1e30
HID = 1e9
F32 = jnp.float32
BF16 = jnp.bfloat16

KV0, WF0, WL0, WS0, QL0, QS0, OO0, OS0, PP0, PW0, COUNT = 0, 8, 16, 19, 21, 24, 28, 35, 42, 49, 56


def dot(a, b, ca, cb):
    return lax.dot_general(a, b, (((ca,), (cb,)), ((), ())), preferred_element_type=F32)


def kernel(
    q_in, k_in, v_in, ok_in, ov_in, ck_in, cv_in, w_in, res_in, gain_in, span_in, mlen_in,
    out_ref,
    kv, qb, wall, kpos, osend, orecv, ssend, srecv, psend, precv, pwsend, pwrecv, attn_s, stream_s,
    ssem, rsem,
):
    ctx = lax.axis_index("ctx")
    dp = lax.axis_index("dp")
    near = lax.rem(ctx, 8)
    far = lax.div(ctx, 8)
    core = lax.rem(near, 2)
    zl = lax.div(near, 2)
    zh = lax.rem(far, 4)
    y = lax.div(far, 4)

    def far_ctx(fy, fz):
        return (fy * 4 + fz) * 8 + near

    def near_ctx(member):
        return far * 8 + member

    zp, zm, zo = lax.rem(zh + 1, 4), lax.rem(zh + 3, 4), lax.rem(zh + 2, 4)
    up, down, other = far_ctx(y, zp), far_ctx(y, zm), far_ctx(1 - y, zh)
    sib = near_ctx(zl * 2 + 1 - core)

    barrier = pltpu.get_barrier_semaphore()
    for peer in (up, down, other):
        pl.semaphore_signal(barrier, inc=1, device_id={"ctx": peer}, device_id_type=MESH)
    for k in range(1, 8):
        pl.semaphore_signal(barrier, inc=1, device_id={"ctx": near_ctx(lax.rem(near + k, 8))}, device_id_type=MESH)
    for k in range(1, 8):
        pl.semaphore_signal(barrier, inc=1, device_id={"dp": lax.rem(dp + k, 8)}, device_id_type=MESH)

    row16 = lax.broadcasted_iota(jnp.int32, (16, 256), 0)
    s0 = span_in[0].astype(F32)
    s1 = span_in[1].astype(F32)
    pick_r = lax.broadcasted_iota(jnp.int32, (16, 32), 0)
    pick_c = lax.broadcasted_iota(jnp.int32, (16, 32), 1)
    for half, (new, old, conv) in enumerate(((k_in, ok_in, ck_in), (v_in, ov_in, cv_in))):
        kv[far, half, 0:128, :] = new[...]
        rows = old[...]
        heads = []
        taps = []
        for t in range(4):
            pick = jnp.where(pick_c == pick_r * 4 + t, 1.0, 0.0).astype(BF16)
            taps.append(dot(pick, rows, 1, 0).astype(BF16))
        for h in range(2):
            total = jnp.zeros((16, 128), F32)
            for t in range(4):
                total = total + dot(taps[t][:, h * 128 : (h + 1) * 128], conv[h, t], 1, 0)
            heads.append(total)
        mem = jnp.concatenate(heads, axis=1)
        if half == 0:
            mem = jnp.where(row16 == 8, s0, jnp.where(row16 == 9, s1, mem))
        kv[far, half, 128:144, :] = mem.astype(BF16)
    qb[near, 0:128, :] = q_in[...]
    qb[near, 128:144, :] = jnp.where(row16 == 0, s0, jnp.where(row16 == 1, s1, 0.0)).astype(BF16)
    wall[far, zl, core] = w_in[...]

    pl.semaphore_wait(barrier, 17)

    def copy(number, ref, dst, where):
        return pltpu.make_async_remote_copy(
            src_ref=ref, dst_ref=dst, send_sem=ssem.at[number], recv_sem=rsem.at[number],
            device_id=where, device_id_type=MESH,
        )

    def same(number, ref, where):
        return copy(number, ref, ref, {"ctx": where})

    def kv_of(fy, fz, part):
        block = kv.at[fy * 4 + fz]
        return block if part is None else block.at[part]

    def w_of(fy, fz, part):
        if part is None:
            return wall.at[fy * 4 + fz, :, core]
        return wall.at[fy * 4 + fz, pl.ds(part * 2, 2), core]

    def send_far(base, of, step):
        for s in step:
            if s == 0:
                same(base, of(y, zh, None), up).start()
            if s == 1:
                same(base + 1, of(y, zh, None), down).start()
            if s == 2:
                same(base + 2, of(y, zh, None), other).start()
            if s == 3:
                same(base + 3, of(y, zm, 0), up).start()
            if s == 4:
                same(base + 4, of(y, zp, 1), down).start()
            if s == 5:
                same(base + 5, of(y, zm, None), other).start()
            if s == 6:
                same(base + 6, of(y, zp, None), other).start()
            if s == 7:
                same(base + 7, of(y, zo, None), other).start()

    def landed(base, of, step):
        blocks = {
            0: (y, zm, None), 1: (y, zp, None), 2: (1 - y, zh, None), 3: (y, zo, 0),
            4: (y, zo, 1), 5: (1 - y, zm, None), 6: (1 - y, zp, None), 7: (1 - y, zo, None),
        }
        for s in step:
            same(base + s, of(*blocks[s]), other).wait_recv()

    send_far(KV0, kv_of, (0, 1, 2))
    for k in (1, 2, 3):
        same(WL0 + k - 1, wall.at[far, zl, core], near_ctx(lax.rem(zl + k, 4) * 2 + core)).start()
    for k in (1, 2, 3):
        same(QL0 + k - 1, qb.at[near], near_ctx(lax.rem(zl + k, 4) * 2 + core)).start()
    same(QS0, qb.at[near], sib).start()

    for k in (1, 2, 3):
        src = lax.rem(zl + 4 - k, 4)
        same(QL0 + k - 1, qb.at[src * 2 + core], sib).wait_recv()
        same(QS0 + k, qb.at[src * 2 + core], sib).start()

    landed(KV0, kv_of, (0,))
    send_far(KV0, kv_of, (3, 5))
    landed(KV0, kv_of, (1,))
    send_far(KV0, kv_of, (4, 6))
    for k in (1, 2, 3):
        same(WL0 + k - 1, wall.at[far, lax.rem(zl + 4 - k, 4), core], sib).wait_recv()
    send_far(WF0, w_of, (0, 1, 2))
    landed(KV0, kv_of, (3, 4))
    send_far(KV0, kv_of, (7,))
    landed(KV0, kv_of, (2, 5, 6, 7))
    same(QS0, qb.at[zl * 2 + 1 - core], sib).wait_recv()
    for k in (1, 2, 3):
        same(QS0 + k, qb.at[lax.rem(zl + 4 - k, 4) * 2 + 1 - core], sib).wait_recv()

    r = lax.broadcasted_iota(jnp.int32, (144, 128), 0)
    rf = r.astype(F32)
    first = (512 - mlen_in[0]).astype(F32)
    for f in range(8):
        tail = kv[f, 0, 128:144, 0:128].astype(F32)
        slot = rf - 128.0 + ((f * 8 + near) * 8).astype(F32)
        mem_pos = jnp.where((slot >= first) & (r < 136), -1.0, HID)
        low = jnp.broadcast_to(tail[8:9] * 64.0, (144, 128)) + rf
        high = jnp.broadcast_to(tail[9:10] * 64.0 - 64.0, (144, 128)) + rf
        kpos[f] = jnp.where(r < 64, low, jnp.where(r < 128, high, mem_pos))

    factor = math.log2(math.e) / math.sqrt(128.0)
    lane = lax.broadcasted_iota(jnp.int32, (8, 128), 1)
    row8 = lax.broadcasted_iota(jnp.int32, (8, 128), 0)

    def attend(m, o_ref, s_ref):
        tail = qb[m, 128:144, 0:128].astype(F32)
        qs0 = jnp.broadcast_to(tail[0:1], (8, 128))
        qs1 = jnp.broadcast_to(tail[1:2], (8, 128))
        qpos = jnp.where(lane < 64, qs0 * 64.0, qs1 * 64.0 - 64.0) + lane.astype(F32)
        vis = kpos[...].reshape(1152, 128) <= qpos[0:1]
        stats = jnp.zeros((8, 128), F32)
        for h in range(2):
            cols = slice(h * 128, (h + 1) * 128)
            keys = kv[:, 0, :, cols].reshape(1152, 128)
            vals = kv[:, 1, :, cols].reshape(1152, 128)
            s = dot(keys, qb[m, 0:128, cols], 1, 1) * factor
            s = jnp.where(vis, s, NEG)
            top = jnp.max(s, axis=0, keepdims=True)
            p = jnp.where(vis, jnp.exp2(s - top), 0.0)
            total = jnp.sum(p, axis=0, keepdims=True)
            o_ref[m if o_ref is osend else near, cols, :] = dot(vals, p.astype(BF16), 0, 0).astype(BF16)
            stats = jnp.where(row8 == h, top, jnp.where(row8 == h + 2, total, stats))
        s_ref[m if s_ref is ssend else near] = stats

    def one(k, carry):
        m = lax.rem(near + k, 8)
        attend(m, osend, ssend)
        copy(OO0 + k - 1, osend.at[m], orecv.at[near], {"ctx": near_ctx(m)}).start()
        copy(OS0 + k - 1, ssend.at[m], srecv.at[near], {"ctx": near_ctx(m)}).start()
        return carry

    lax.fori_loop(1, 5, one, 0)
    landed(WF0, w_of, (0,))
    send_far(WF0, w_of, (3, 5))
    landed(WF0, w_of, (1,))
    send_far(WF0, w_of, (4, 6))
    lax.fori_loop(5, 8, one, 0)
    attend(near, orecv, srecv)

    landed(WF0, w_of, (3, 4))
    send_far(WF0, w_of, (7,))

    def w_half(fy, c):
        return wall.at[pl.ds(fy * 4, 4), :, c]

    same(WS0, w_half(y, core), sib).start()
    landed(WF0, w_of, (2, 5, 6, 7))
    same(WS0 + 1, w_half(1 - y, core), sib).start()

    for k in range(1, 8):
        src = lax.rem(near + 8 - k, 8)
        copy(OO0 + k - 1, osend.at[src], orecv.at[src], {"ctx": sib}).wait_recv()
        copy(OS0 + k - 1, ssend.at[src], srecv.at[src], {"ctx": sib}).wait_recv()

    for h in range(2):
        cols = slice(h * 128, (h + 1) * 128)
        tops = srecv[:, h, :]
        sums = srecv[:, h + 2, :]
        best = jnp.max(tops, axis=0, keepdims=True)
        weight = jnp.exp2(tops - best)
        total = jnp.sum(weight * sums, axis=0, keepdims=True)
        acc = jnp.zeros((128, 128), F32)
        for j in range(8):
            acc = acc + orecv[j, cols, :].astype(F32) * weight[j : j + 1]
        attn_s[:, cols] = (acc / total).T.astype(BF16)

    same(WS0, w_half(y, 1 - core), sib).wait_recv()
    same(WS0 + 1, w_half(1 - y, 1 - core), sib).wait_recv()

    def project(g):
        return dot(attn_s[...], wall[g].reshape(512, 256), 1, 1)

    def push(k, carry):
        g = lax.rem(dp + k, 8)
        psend[g] = project(g).astype(BF16)
        copy(PP0 + k - 1, psend.at[g], precv.at[dp], {"dp": g}).start()
        return carry

    lax.fori_loop(1, 8, push, 0)
    stream_s[...] = res_in[...].astype(F32) + project(dp)
    for k in range(1, 8):
        src = lax.rem(dp + 8 - k, 8)
        copy(PP0 + k - 1, psend.at[src], precv.at[src], {"dp": src}).wait_recv()
        stream_s[...] += precv[src].astype(F32)

    stream = stream_s[...]
    mine = jnp.sum(stream * stream, axis=1, keepdims=True)
    line = jnp.broadcast_to(mine, (128, 128)).T
    pwsend[...] = line[0:8]
    pwrecv[dp] = line[0:8]
    for k in range(1, 8):
        copy(PW0 + k - 1, pwsend, pwrecv.at[dp], {"dp": lax.rem(dp + k, 8)}).start()
    for k in range(1, 8):
        src = lax.rem(dp + 8 - k, 8)
        copy(PW0 + k - 1, pwsend, pwrecv.at[src], {"dp": src}).wait_recv()
    power = jnp.sum(pwrecv[...], axis=0)[0:1] / 4096.0
    norm = jnp.broadcast_to(lax.rsqrt(power + 1e-6), (128, 128)).T
    gain = gain_in[...].astype(F32)
    for c in range(4):
        cols = slice(c * 128, (c + 1) * 128)
        out_ref[:, cols] = (stream_s[:, cols] * norm * gain[:, cols]).astype(BF16)

    for s in range(8):
        whole = s not in (3, 4)
        same(KV0 + s, kv_of(y, zh, None if whole else 0), other).wait_send()
        same(WF0 + s, w_of(y, zh, None if whole else 0), other).wait_send()
    for k in range(3):
        same(WL0 + k, wall.at[far, zl, core], sib).wait_send()
        same(QL0 + k, qb.at[near], sib).wait_send()
    for k in range(4):
        same(QS0 + k, qb.at[near], sib).wait_send()
    same(WS0, w_half(y, core), sib).wait_send()
    same(WS0 + 1, w_half(1 - y, core), sib).wait_send()
    for k in range(7):
        copy(OO0 + k, osend.at[0], orecv.at[near], {"ctx": sib}).wait_send()
        copy(OS0 + k, ssend.at[0], srecv.at[near], {"ctx": sib}).wait_send()
        copy(PP0 + k, psend.at[0], precv.at[dp], {"ctx": sib}).wait_send()
        copy(PW0 + k, pwsend, pwrecv.at[dp], {"ctx": sib}).wait_send()


def local(
    queries, keys, values, old_keys, old_values, conv_keys, conv_values, out_proj, residual, gain,
    span_order, memory_length,
):
    vm = pl.BlockSpec(memory_space=pltpu.VMEM)
    sm = pl.BlockSpec(memory_space=pltpu.SMEM)
    return pl.pallas_call(
        kernel,
        out_shape=jax.ShapeDtypeStruct(residual.shape, BF16),
        in_specs=[vm] * 10 + [sm] * 2,
        out_specs=vm,
        scratch_shapes=[
            pltpu.VMEM((8, 2, 144, 256), BF16),
            pltpu.VMEM((8, 144, 256), BF16),
            pltpu.VMEM((8, 4, 2, 64, 256), BF16),
            pltpu.VMEM((8, 144, 128), F32),
            pltpu.VMEM((8, 256, 128), BF16),
            pltpu.VMEM((8, 256, 128), BF16),
            pltpu.VMEM((8, 8, 128), F32),
            pltpu.VMEM((8, 8, 128), F32),
            pltpu.VMEM((8, 128, 512), BF16),
            pltpu.VMEM((8, 128, 512), BF16),
            pltpu.VMEM((8, 128), F32),
            pltpu.VMEM((8, 8, 128), F32),
            pltpu.VMEM((128, 256), BF16),
            pltpu.VMEM((128, 512), F32),
            pltpu.SemaphoreType.DMA((COUNT,)),
            pltpu.SemaphoreType.DMA((COUNT,)),
        ],
        compiler_params=pltpu.CompilerParams(collective_id=0, has_side_effects=True),
    )(
        queries, keys, values, old_keys, old_values, conv_keys, conv_values, out_proj, residual,
        gain.reshape(1, -1), span_order, memory_length,
    )


def solution(mesh):
    placed = (
        P("ctx", "dp"),
        P("ctx", "dp"),
        P("ctx", "dp"),
        P("ctx", "dp"),
        P("ctx", "dp"),
        P("dp", None, None, None),
        P("dp", None, None, None),
        P("ctx", "dp"),
        P("ctx", "dp"),
        P("dp"),
        P("ctx"),
        P(),
    )
    return jax.shard_map(
        local, mesh=mesh, in_specs=placed, out_specs=P("ctx", "dp"), check_vma=False
    )
```

time: 804 us -> 110 us (0.14)
  the two profiles are of different devices: /device:TPU:1 before, /device:TPU:32 now
where the time goes in v1:
time: 110 us; the launch traced here: 109 us
  Pallas kernels  107 us (97%)
  local copies, waits for them, and re-layouts  2.16 us (2%)
    pallas_call x1, Pallas kernels, local(): pl.pallas_call(kernel, out_shape=jax.ShapeDtypeStruct(residual.shape, BF1...  107 us

profile of v1, /device:TPU:32, one launch (start us, length us, event | category | flops | bytes accessed | tf_op | source)
XLA Modules:
  0.0 109.4 jit_solution(6202955040020090465)
XLA Ops:
  0.0 0.0 copy-start
  0.7 0.0 copy-done
  0.7 0.6 reshape.3.gain_in
  1.3 106.5 %shard_map.118 = bf16[128,512]{1,0:T(8,128)(2,1)} custom-call(bf16[128,256]{1,0:T(8,128)(2,1)} %q_in.1, bf16[128,256]{1,0:T(8,128)(2,1)} %k_in.1, bf16[128,256]{1,0:T(8,128)(2,1)} %v_in.1, bf16[32,256]{1,0:T(8,128)(2,1)} %ok_in.1, bf16[32,256]{1,0:T(8,128)(2,1)} %ov_in.1, bf16[2,4,128,128]{3,2,1,0:T(8,128)(2,1)} %ck_in.1, bf16[2,4,128,128]{3,2,1,0:T(8,128)(2,1)} %cv_in.1, ...), custom_call_target="tpu_custom_call" | custom-call | tf_op jit(solution)/shard_map/pallas_call | solution.py:292
  107.8 1.6 %copy.15 = bf16[128,512]{1,0:T(8,128)(2,1)} copy(bf16[128,512]{1,0:T(8,128)(2,1)} %shard_map.118) | data formatting | bytes 262144
Async XLA Ops:
  0.0 0.7 copy-start

commit v2 on v1

v2 whole, which is shorter than its diff:
```python
import math

import jax
import jax.numpy as jnp
from jax import lax
from jax.experimental import pallas as pl
from jax.experimental.pallas import tpu as pltpu
from jax.sharding import PartitionSpec as P

MESH = pl.DeviceIdType.MESH
NEG = -1e30
HID = 1e9
F32 = jnp.float32
BF16 = jnp.bfloat16

KU, KD, VU, VD, WU, WD = 0, 8, 16, 24, 32, 40
SU, SD, SX, QQ, WY, OO, OS, PP, PW, COUNT = 48, 56, 64, 66, 69, 70, 73, 76, 83, 90


def dot(a, b, ca, cb):
    return lax.dot_general(a, b, (((ca,), (cb,)), ((), ())), preferred_element_type=F32)


def kernel(
    q_in, k_in, v_in, ok_in, ov_in, ck_in, cv_in, w_in, res_in, gain_in, span_in, mlen_in,
    out_ref,
    kv, qb, wall, acc, rows, osend, orecv, ssend, srecv, psend, precv, pwsend, pwrecv, attn_s, stream_s,
    ssem, rsem,
):
    ctx = lax.axis_index("ctx")
    dp = lax.axis_index("dp")
    core = lax.rem(ctx, 2)
    z = lax.rem(lax.div(ctx, 2), 16)
    y = lax.div(ctx, 32)
    me = y * 2 + core

    def at(fy, fz, fc):
        return (fy * 16 + fz) * 2 + fc

    def behind(s):
        return lax.rem(z + 16 - s, 16)

    def ahead(s):
        return lax.rem(z + s, 16)

    up, down = at(y, ahead(1), core), at(y, behind(1), core)
    sib, other, cross = at(y, z, 1 - core), at(1 - y, z, core), at(1 - y, z, 1 - core)

    barrier = pltpu.get_barrier_semaphore()
    for peer in (up, down, sib, other, cross):
        pl.semaphore_signal(barrier, inc=1, device_id={"ctx": peer}, device_id_type=MESH)
    for k in range(1, 8):
        pl.semaphore_signal(barrier, inc=1, device_id={"dp": lax.rem(dp + k, 8)}, device_id_type=MESH)

    row16 = lax.broadcasted_iota(jnp.int32, (16, 256), 0)
    s0 = span_in[0].astype(F32)
    s1 = span_in[1].astype(F32)
    pick_r = lax.broadcasted_iota(jnp.int32, (16, 32), 0)
    pick_c = lax.broadcasted_iota(jnp.int32, (16, 32), 1)
    for half, (new, old, conv) in enumerate(((k_in, ok_in, ck_in), (v_in, ov_in, cv_in))):
        kv[z, half, 0:128, :] = new[...]
        taps = []
        for t in range(4):
            pick = jnp.where(pick_c == pick_r * 4 + t, 1.0, 0.0).astype(BF16)
            taps.append(dot(pick, old[...], 1, 0).astype(BF16))
        heads = []
        for h in range(2):
            total = jnp.zeros((16, 128), F32)
            for t in range(4):
                total = total + dot(taps[t][:, h * 128 : (h + 1) * 128], conv[h, t], 1, 0)
            heads.append(total)
        mem = jnp.concatenate(heads, axis=1)
        if half == 0:
            mem = jnp.where(row16 == 8, s0, jnp.where(row16 == 9, s1, mem))
        kv[z, half, 128:144, :] = mem.astype(BF16)
    qb[me, 0:128, :] = q_in[...]
    qb[me, 128:144, :] = jnp.where(row16 == 0, s0, jnp.where(row16 == 1, s1, 0.0)).astype(BF16)
    wall[y, z, core] = w_in[...]
    acc[...] = jnp.zeros_like(acc)
    rows[...] = jnp.where(lax.broadcasted_iota(jnp.int32, (8, 512), 0) < 2, NEG, 0.0)

    pl.semaphore_wait(barrier, 12)

    def copy(number, ref, dst, where):
        return pltpu.make_async_remote_copy(
            src_ref=ref, dst_ref=dst, send_sem=ssem.at[number], recv_sem=rsem.at[number],
            device_id=where, device_id_type=MESH,
        )

    def same(number, ref, where):
        return copy(number, ref, ref, {"ctx": where})

    def w_of(fz, c):
        return wall.at[:, fz, c]

    same(WY, wall.at[y, z, core], other).start()
    same(KU, kv.at[z, 0], up).start()
    same(KD, kv.at[z, 0], down).start()
    for k, peer in enumerate((other, cross, sib)):
        same(QQ + k, qb.at[me], peer).start()
    same(VU, kv.at[z, 1], up).start()
    same(VD, kv.at[z, 1], down).start()
    same(WY, wall.at[1 - y, z, core], other).wait_recv()
    same(WU, w_of(z, core), up).start()
    same(WD, w_of(z, core), down).start()
    same(SX, w_of(z, core), sib).start()
    for k, (fy, fc) in enumerate(((1 - y, core), (1 - y, 1 - core), (y, 1 - core))):
        same(QQ + k, qb.at[fy * 2 + fc], other).wait_recv()

    factor = math.log2(math.e) / math.sqrt(128.0)
    r = lax.broadcasted_iota(jnp.int32, (144, 128), 0)
    rf = r.astype(F32)
    first = (512 - mlen_in[0]).astype(F32)
    lane = lax.broadcasted_iota(jnp.int32, (8, 128), 1)

    def positions(fz):
        tail = kv[fz, 0, 128:144, 0:128].astype(F32)
        slot = rf - 128.0 + (at(y, fz, core) * 8).astype(F32)
        mem_pos = jnp.where((slot >= first) & (r < 136), -1.0, HID)
        low = jnp.broadcast_to(tail[8:9] * 64.0, (144, 128)) + rf
        high = jnp.broadcast_to(tail[9:10] * 64.0 - 64.0, (144, 128)) + rf
        place = jnp.where(r < 64, low, jnp.where(r < 128, high, mem_pos))
        return jnp.concatenate([place] * 4, axis=1)

    def fold(blocks):
        parts = []
        for m in range(4):
            tail = qb[m, 128:144, 0:128].astype(F32)
            q0 = jnp.broadcast_to(tail[0:1], (8, 128))
            q1 = jnp.broadcast_to(tail[1:2], (8, 128))
            parts.append(jnp.where(lane < 64, q0 * 64.0, q1 * 64.0 - 64.0) + lane.astype(F32))
        qpos = jnp.concatenate(parts, axis=1)[0:1]
        vis = jnp.concatenate([positions(b) for b in blocks], axis=0) <= qpos
        for h in range(2):
            cols = slice(h * 128, (h + 1) * 128)
            keys = jnp.concatenate([kv[b, 0, :, cols] for b in blocks], axis=0)
            vals = jnp.concatenate([kv[b, 1, :, cols] for b in blocks], axis=0)
            s = dot(keys, qb[:, 0:128, cols].reshape(512, 128), 1, 1) * factor
            s = jnp.where(vis, s, NEG)
            before = rows[h : h + 1, :]
            top = jnp.maximum(before, jnp.max(s, axis=0, keepdims=True))
            p = jnp.where(vis, jnp.exp2(s - top), 0.0)
            shrink = jnp.exp2(before - top)
            rows[h : h + 1, :] = top
            rows[h + 2 : h + 3, :] = rows[h + 2 : h + 3, :] * shrink + jnp.sum(p, axis=0, keepdims=True)
            acc[cols, :] = acc[cols, :] * shrink + dot(vals, p.astype(BF16), 0, 0)

    fold([z])

    def stage(s, carry):
        lo, hi = behind(s), ahead(s)
        for base, half, at_z, to in ((KU, 0, lo, up), (KD, 0, hi, down), (VU, 1, lo, up), (VD, 1, hi, down)):
            same(base + s - 1, kv.at[at_z, half], to).wait_recv()
            same(base + s, kv.at[at_z, half], to).start()
        fold([lo, hi])
        for base, side, at_z, to in ((WU, SU, lo, up), (WD, SD, hi, down)):
            same(base + s - 1, w_of(at_z, core), to).wait_recv()
            same(base + s, w_of(at_z, core), to).start()
            same(side + s - 1, w_of(at_z, core), sib).start()
        return carry

    lax.fori_loop(1, 7, stage, 0)
    lo, hi, far = behind(7), ahead(7), ahead(8)
    for base, half, at_z, to in ((KU, 0, lo, up), (KD, 0, hi, down), (VU, 1, lo, up), (VD, 1, hi, down)):
        same(base + 6, kv.at[at_z, half], to).wait_recv()
        if base in (KU, VD):
            same(base + 7, kv.at[at_z, half], to).start()
    fold([lo, hi])
    for base, side, at_z, to, fy in ((WU, SU, lo, up, 0), (WD, SD, hi, down, 1)):
        same(base + 6, w_of(at_z, core), to).wait_recv()
        same(base + 7, wall.at[fy, at_z, core], to).start()
        same(side + 6, w_of(at_z, core), sib).start()
    same(KU + 7, kv.at[far, 0], up).wait_recv()
    same(VD + 7, kv.at[far, 1], down).wait_recv()
    fold([far])

    for k, (fy, fc) in enumerate(((1 - y, core), (1 - y, 1 - core), (y, 1 - core))):
        m = fy * 2 + fc
        peer = (other, cross, sib)[k]
        lanes = pl.ds(pl.multiple_of(m * 128, 128), 128)
        osend[k] = acc[:, lanes].astype(BF16)
        ssend[k] = rows[:, lanes]
        copy(OO + k, osend.at[k], orecv.at[k], {"ctx": peer}).start()
        copy(OS + k, ssend.at[k], srecv.at[k], {"ctx": peer}).start()
    lanes = pl.ds(pl.multiple_of(me * 128, 128), 128)
    srecv[3] = rows[:, lanes]

    for base, fy in ((WU, 0), (WD, 1)):
        same(base + 7, wall.at[fy, far, core], up).wait_recv()
    same(SX + 1, w_of(far, core), sib).start()

    for k in range(3):
        copy(OO + k, osend.at[k], orecv.at[k], {"ctx": sib}).wait_recv()
        copy(OS + k, ssend.at[k], srecv.at[k], {"ctx": sib}).wait_recv()
    for h in range(2):
        cols = slice(h * 128, (h + 1) * 128)
        tops = srecv[:, h, :]
        sums = srecv[:, h + 2, :]
        best = jnp.max(tops, axis=0, keepdims=True)
        weight = jnp.exp2(tops - best)
        total = jnp.sum(weight * sums, axis=0, keepdims=True)
        mixed = acc[cols, lanes] * weight[3:4]
        for j in range(3):
            mixed = mixed + orecv[j, cols, :].astype(F32) * weight[j : j + 1]
        attn_s[:, cols] = (mixed / total).T.astype(BF16)

    for s in range(1, 8):
        same(SU + s - 1, w_of(behind(s), 1 - core), sib).wait_recv()
        same(SD + s - 1, w_of(ahead(s), 1 - core), sib).wait_recv()
    same(SX, w_of(z, 1 - core), sib).wait_recv()
    same(SX + 1, w_of(far, 1 - core), sib).wait_recv()

    def project(g):
        block = wall[lax.div(g, 4), pl.ds(lax.rem(g, 4) * 4, 4)]
        return dot(attn_s[...], block.reshape(512, 256), 1, 1)

    def push(k, carry):
        g = lax.rem(dp + k, 8)
        psend[g] = project(g).astype(BF16)
        copy(PP + k - 1, psend.at[g], precv.at[dp], {"dp": g}).start()
        return carry

    lax.fori_loop(1, 8, push, 0)
    stream_s[...] = res_in[...].astype(F32) + project(dp)
    for k in range(1, 8):
        src = lax.rem(dp + 8 - k, 8)
        copy(PP + k - 1, psend.at[src], precv.at[src], {"dp": src}).wait_recv()
        stream_s[...] += precv[src].astype(F32)

    stream = stream_s[...]
    mine = jnp.sum(stream * stream, axis=1, keepdims=True)
    line = jnp.broadcast_to(mine, (128, 128)).T
    pwsend[...] = line[0:8]
    pwrecv[dp] = line[0:8]
    for k in range(1, 8):
        copy(PW + k - 1, pwsend, pwrecv.at[dp], {"dp": lax.rem(dp + k, 8)}).start()
    for k in range(1, 8):
        src = lax.rem(dp + 8 - k, 8)
        copy(PW + k - 1, pwsend, pwrecv.at[src], {"dp": src}).wait_recv()
    power = jnp.sum(pwrecv[...], axis=0)[0:1] / 4096.0
    norm = jnp.broadcast_to(lax.rsqrt(power + 1e-6), (128, 128)).T
    gain = gain_in[...].astype(F32)
    for c in range(4):
        cols = slice(c * 128, (c + 1) * 128)
        out_ref[:, cols] = (stream_s[:, cols] * norm * gain[:, cols]).astype(BF16)

    for s in range(8):
        if s < 7:
            same(VU + s, kv.at[z, 1], up).wait_send()
            same(KD + s, kv.at[z, 0], up).wait_send()
            same(SU + s, w_of(z, core), sib).wait_send()
            same(SD + s, w_of(z, core), sib).wait_send()
        same(KU + s, kv.at[z, 0], up).wait_send()
        same(VD + s, kv.at[z, 1], up).wait_send()
        for base in (WU, WD):
            same(base + s, w_of(z, core) if s < 7 else wall.at[0, z, core], up).wait_send()
    same(SX, w_of(z, core), sib).wait_send()
    same(SX + 1, w_of(z, core), sib).wait_send()
    same(WY, wall.at[y, z, core], other).wait_send()
    for k in range(3):
        same(QQ + k, qb.at[me], sib).wait_send()
        copy(OO + k, osend.at[k], orecv.at[k], {"ctx": sib}).wait_send()
        copy(OS + k, ssend.at[k], srecv.at[k], {"ctx": sib}).wait_send()
    for k in range(7):
        copy(PP + k, psend.at[0], precv.at[dp], {"ctx": sib}).wait_send()
        copy(PW + k, pwsend, pwrecv.at[dp], {"ctx": sib}).wait_send()


def local(
    queries, keys, values, old_keys, old_values, conv_keys, conv_values, out_proj, residual, gain,
    span_order, memory_length,
):
    vm = pl.BlockSpec(memory_space=pltpu.VMEM)
    sm = pl.BlockSpec(memory_space=pltpu.SMEM)
    return pl.pallas_call(
        kernel,
        out_shape=jax.ShapeDtypeStruct(residual.shape, BF16),
        in_specs=[vm] * 10 + [sm] * 2,
        out_specs=vm,
        scratch_shapes=[
            pltpu.VMEM((16, 2, 144, 256), BF16),
            pltpu.VMEM((4, 144, 256), BF16),
            pltpu.VMEM((2, 16, 2, 64, 256), BF16),
            pltpu.VMEM((256, 512), F32),
            pltpu.VMEM((8, 512), F32),
            pltpu.VMEM((3, 256, 128), BF16),
            pltpu.VMEM((3, 256, 128), BF16),
            pltpu.VMEM((3, 8, 128), F32),
            pltpu.VMEM((4, 8, 128), F32),
            pltpu.VMEM((8, 128, 512), BF16),
            pltpu.VMEM((8, 128, 512), BF16),
            pltpu.VMEM((8, 128), F32),
            pltpu.VMEM((8, 8, 128), F32),
            pltpu.VMEM((128, 256), BF16),
            pltpu.VMEM((128, 512), F32),
            pltpu.SemaphoreType.DMA((COUNT,)),
            pltpu.SemaphoreType.DMA((COUNT,)),
        ],
        compiler_params=pltpu.CompilerParams(collective_id=0, has_side_effects=True),
    )(
        queries, keys, values, old_keys, old_values, conv_keys, conv_values, out_proj, residual,
        gain.reshape(1, -1), span_order, memory_length,
    )


def solution(mesh):
    placed = (
        P("ctx", "dp"),
        P("ctx", "dp"),
        P("ctx", "dp"),
        P("ctx", "dp"),
        P("ctx", "dp"),
        P("dp", None, None, None),
        P("dp", None, None, None),
        P("ctx", "dp"),
        P("ctx", "dp"),
        P("dp"),
        P("ctx"),
        P(),
    )
    return jax.shard_map(
        local, mesh=mesh, in_specs=placed, out_specs=P("ctx", "dp"), check_vma=False
    )
```

time: 110 us -> 85.7 us (0.78)
  the two profiles are of different devices: /device:TPU:32 before, /device:TPU:1 now
where the time goes in v2:
time: 85.7 us; the launch traced here: 85.3 us
  Pallas kernels  82.5 us (96%)
  local copies, waits for them, and re-layouts  2.16 us (3%)
    pallas_call x1, Pallas kernels, local(): pl.pallas_call(kernel, out_shape=jax.ShapeDtypeStruct(residual.shape, BF1...  82.5 us

profile of v2, /device:TPU:1, one launch (start us, length us, event | category | flops | bytes accessed | tf_op | source)
XLA Modules:
  0.0 85.3 jit_solution(3458695720121240137)
XLA Ops:
  0.0 0.0 copy-start
  0.7 0.0 copy-done
  0.7 0.6 reshape.3.gain_in
  1.3 82.5 %shard_map.118 = bf16[128,512]{1,0:T(8,128)(2,1)} custom-call(bf16[128,256]{1,0:T(8,128)(2,1)} %q_in.1, bf16[128,256]{1,0:T(8,128)(2,1)} %k_in.1, bf16[128,256]{1,0:T(8,128)(2,1)} %v_in.1, bf16[32,256]{1,0:T(8,128)(2,1)} %ok_in.1, bf16[32,256]{1,0:T(8,128)(2,1)} %ov_in.1, bf16[2,4,128,128]{3,2,1,0:T(8,128)(2,1)} %ck_in.1, bf16[2,4,128,128]{3,2,1,0:T(8,128)(2,1)} %cv_in.1, ...), custom_call_target="tpu_custom_call" | custom-call | tf_op jit(solution)/shard_map/pallas_call | solution.py:275
  83.7 1.6 %copy.15 = bf16[128,512]{1,0:T(8,128)(2,1)} copy(bf16[128,512]{1,0:T(8,128)(2,1)} %shard_map.118) | data formatting | bytes 262144
Async XLA Ops:
  0.0 0.7 copy-start

commit v3 on v2

--- a/solution.py
+++ b/solution.py
@@ -13,8 +13,8 @@
 F32 = jnp.float32
 BF16 = jnp.bfloat16
 
-KU, KD, VU, VD, WU, WD = 0, 8, 16, 24, 32, 40
-SU, SD, SX, QQ, WY, OO, OS, PP, PW, COUNT = 48, 56, 64, 66, 69, 70, 73, 76, 83, 90
+KU, KD, WU, WD, SU, SD, SX, QQ, WY = 0, 32, 64, 72, 80, 88, 96, 98, 101
+OO, OS, PW, RL, RF, PD, COUNT = 102, 105, 108, 115, 119, 123, 128
 
 
 def dot(a, b, ca, cb):
@@ -24,7 +24,7 @@
 def kernel(
     q_in, k_in, v_in, ok_in, ov_in, ck_in, cv_in, w_in, res_in, gain_in, span_in, mlen_in,
     out_ref,
-    kv, qb, wall, acc, rows, osend, orecv, ssend, srecv, psend, precv, pwsend, pwrecv, attn_s, stream_s,
+    kv, qb, wall, acc, rows, osend, orecv, ssend, srecv, psend, precv, relay, pwsend, pwrecv, attn_s, stream_s,
     ssem, rsem,
 ):
     ctx = lax.axis_index("ctx")
@@ -58,7 +58,8 @@
     pick_r = lax.broadcasted_iota(jnp.int32, (16, 32), 0)
     pick_c = lax.broadcasted_iota(jnp.int32, (16, 32), 1)
     for half, (new, old, conv) in enumerate(((k_in, ok_in, ck_in), (v_in, ov_in, cv_in))):
-        kv[z, half, 0:128, :] = new[...]
+        for h in range(2):
+            kv[z, half * 2 + h, 0:128, :] = new[:, h * 128 : (h + 1) * 128]
         taps = []
         for t in range(4):
             pick = jnp.where(pick_c == pick_r * 4 + t, 1.0, 0.0).astype(BF16)
@@ -72,7 +73,8 @@
         mem = jnp.concatenate(heads, axis=1)
         if half == 0:
             mem = jnp.where(row16 == 8, s0, jnp.where(row16 == 9, s1, mem))
-        kv[z, half, 128:144, :] = mem.astype(BF16)
+        for h in range(2):
+            kv[z, half * 2 + h, 128:144, :] = mem[:, h * 128 : (h + 1) * 128].astype(BF16)
     qb[me, 0:128, :] = q_in[...]
     qb[me, 128:144, :] = jnp.where(row16 == 0, s0, jnp.where(row16 == 1, s1, 0.0)).astype(BF16)
     wall[y, z, core] = w_in[...]
@@ -94,12 +96,14 @@
         return wall.at[:, fz, c]
 
     same(WY, wall.at[y, z, core], other).start()
-    same(KU, kv.at[z, 0], up).start()
-    same(KD, kv.at[z, 0], down).start()
+    for c in (0, 1):
+        same(KU + c * 8, kv.at[z, c], up).start()
+        same(KD + c * 8, kv.at[z, c], down).start()
     for k, peer in enumerate((other, cross, sib)):
         same(QQ + k, qb.at[me], peer).start()
-    same(VU, kv.at[z, 1], up).start()
-    same(VD, kv.at[z, 1], down).start()
+    for c in (2, 3):
+        same(KU + c * 8, kv.at[z, c], up).start()
+        same(KD + c * 8, kv.at[z, c], down).start()
     same(WY, wall.at[1 - y, z, core], other).wait_recv()
     same(WU, w_of(z, core), up).start()
     same(WD, w_of(z, core), down).start()
@@ -114,7 +118,7 @@
     lane = lax.broadcasted_iota(jnp.int32, (8, 128), 1)
 
     def positions(fz):
-        tail = kv[fz, 0, 128:144, 0:128].astype(F32)
+        tail = kv[fz, 0, 128:144, :].astype(F32)
         slot = rf - 128.0 + (at(y, fz, core) * 8).astype(F32)
         mem_pos = jnp.where((slot >= first) & (r < 136), -1.0, HID)
         low = jnp.broadcast_to(tail[8:9] * 64.0, (144, 128)) + rf
@@ -133,8 +137,8 @@
         vis = jnp.concatenate([positions(b) for b in blocks], axis=0) <= qpos
         for h in range(2):
             cols = slice(h * 128, (h + 1) * 128)
-            keys = jnp.concatenate([kv[b, 0, :, cols] for b in blocks], axis=0)
-            vals = jnp.concatenate([kv[b, 1, :, cols] for b in blocks], axis=0)
+            keys = jnp.concatenate([kv[b, h] for b in blocks], axis=0)
+            vals = jnp.concatenate([kv[b, 2 + h] for b in blocks], axis=0)
             s = dot(keys, qb[:, 0:128, cols].reshape(512, 128), 1, 1) * factor
             s = jnp.where(vis, s, NEG)
             before = rows[h : h + 1, :]
@@ -149,9 +153,10 @@
 
     def stage(s, carry):
         lo, hi = behind(s), ahead(s)
-        for base, half, at_z, to in ((KU, 0, lo, up), (KD, 0, hi, down), (VU, 1, lo, up), (VD, 1, hi, down)):
-            same(base + s - 1, kv.at[at_z, half], to).wait_recv()
-            same(base + s, kv.at[at_z, half], to).start()
+        for c in range(4):
+            for base, at_z, to in ((KU + c * 8, lo, up), (KD + c * 8, hi, down)):
+                same(base + s - 1, kv.at[at_z, c], to).wait_recv()
+                same(base + s, kv.at[at_z, c], to).start()
         fold([lo, hi])
         for base, side, at_z, to in ((WU, SU, lo, up), (WD, SD, hi, down)):
             same(base + s - 1, w_of(at_z, core), to).wait_recv()
@@ -161,17 +166,18 @@
 
     lax.fori_loop(1, 7, stage, 0)
     lo, hi, far = behind(7), ahead(7), ahead(8)
-    for base, half, at_z, to in ((KU, 0, lo, up), (KD, 0, hi, down), (VU, 1, lo, up), (VD, 1, hi, down)):
-        same(base + 6, kv.at[at_z, half], to).wait_recv()
-        if base in (KU, VD):
-            same(base + 7, kv.at[at_z, half], to).start()
+    for c in range(4):
+        for base, at_z, to in ((KU + c * 8, lo, up), (KD + c * 8, hi, down)):
+            same(base + 6, kv.at[at_z, c], to).wait_recv()
+            if (to is up) == (c % 2 == 0):
+                same(base + 7, kv.at[at_z, c], to).start()
     fold([lo, hi])
     for base, side, at_z, to, fy in ((WU, SU, lo, up, 0), (WD, SD, hi, down, 1)):
         same(base + 6, w_of(at_z, core), to).wait_recv()
         same(base + 7, wall.at[fy, at_z, core], to).start()
         same(side + 6, w_of(at_z, core), sib).start()
-    same(KU + 7, kv.at[far, 0], up).wait_recv()
-    same(VD + 7, kv.at[far, 1], down).wait_recv()
+    for c in range(4):
+        same((KD if c % 2 else KU) + c * 8 + 7, kv.at[far, c], up).wait_recv()
     fold([far])
 
     for k, (fy, fc) in enumerate(((1 - y, core), (1 - y, 1 - core), (y, 1 - core))):
@@ -214,17 +220,37 @@
         block = wall[lax.div(g, 4), pl.ds(lax.rem(g, 4) * 4, 4)]
         return dot(attn_s[...], block.reshape(512, 256), 1, 1)
 
-    def push(k, carry):
-        g = lax.rem(dp + k, 8)
+    px = lax.div(dp, 2)
+    py = lax.rem(dp, 2)
+
+    def dp_at(dx, flip):
+        return lax.rem(px + 4 + dx, 4) * 2 + (1 - py if flip else py)
+
+    for flip in (0, 1):
+        g = dp_at(2, flip)
         psend[g] = project(g).astype(BF16)
-        copy(PP + k - 1, psend.at[g], precv.at[dp], {"dp": g}).start()
-        return carry
-
-    lax.fori_loop(1, 8, push, 0)
+        for way, dx in ((0, 1), (1, -1)):
+            copy(RL + way * 2 + flip, psend.at[g, pl.ds(way * 64, 64)], relay.at[way * 2 + flip], {"dp": dp_at(dx, flip)}).start()
+    straight = ((1, 0), (-1, 0), (1, 1), (-1, 1), (0, 1))
+    for n, (dx, flip) in enumerate(straight):
+        g = dp_at(dx, flip)
+        psend[g] = project(g).astype(BF16)
+        copy(PD + n, psend.at[g], precv.at[dp], {"dp": g}).start()
+    for flip in (0, 1):
+        for way, dx in ((0, 1), (1, -1)):
+            n = way * 2 + flip
+            copy(RL + n, relay.at[n], relay.at[n], {"dp": dp_at(dx, 0)}).wait_recv()
+            copy(RF + n, relay.at[n], precv.at[dp_at(-dx, flip), pl.ds(way * 64, 64)], {"dp": dp_at(dx, 0)}).start()
     stream_s[...] = res_in[...].astype(F32) + project(dp)
-    for k in range(1, 8):
-        src = lax.rem(dp + 8 - k, 8)
-        copy(PP + k - 1, psend.at[src], precv.at[src], {"dp": src}).wait_recv()
+    for n, (dx, flip) in enumerate(straight):
+        src = dp_at(-dx, flip)
+        copy(PD + n, psend.at[src], precv.at[src], {"dp": dp_at(1, 0)}).wait_recv()
+        stream_s[...] += precv[src].astype(F32)
+    for flip in (0, 1):
+        src = dp_at(2, flip)
+        for way in (0, 1):
+            n = way * 2 + flip
+            copy(RF + n, relay.at[n], precv.at[src, pl.ds(way * 64, 64)], {"dp": dp_at(1, 0)}).wait_recv()
         stream_s[...] += precv[src].astype(F32)
 
     stream = stream_s[...]
@@ -245,13 +271,13 @@
         out_ref[:, cols] = (stream_s[:, cols] * norm * gain[:, cols]).astype(BF16)
 
     for s in range(8):
+        for c in range(4):
+            for base in (KU, KD):
+                if s < 7 or (base == KU) == (c % 2 == 0):
+                    same(base + c * 8 + s, kv.at[z, c], up).wait_send()
         if s < 7:
-            same(VU + s, kv.at[z, 1], up).wait_send()
-            same(KD + s, kv.at[z, 0], up).wait_send()
             same(SU + s, w_of(z, core), sib).wait_send()
             same(SD + s, w_of(z, core), sib).wait_send()
-        same(KU + s, kv.at[z, 0], up).wait_send()
-        same(VD + s, kv.at[z, 1], up).wait_send()
         for base in (WU, WD):
             same(base + s, w_of(z, core) if s < 7 else wall.at[0, z, core], up).wait_send()
     same(SX, w_of(z, core), sib).wait_send()
@@ -262,8 +288,12 @@
         copy(OO + k, osend.at[k], orecv.at[k], {"ctx": sib}).wait_send()
         copy(OS + k, ssend.at[k], srecv.at[k], {"ctx": sib}).wait_send()
     for k in range(7):
-        copy(PP + k, psend.at[0], precv.at[dp], {"ctx": sib}).wait_send()
         copy(PW + k, pwsend, pwrecv.at[dp], {"ctx": sib}).wait_send()
+    for n in range(4):
+        copy(RL + n, relay.at[n], relay.at[n], {"ctx": sib}).wait_send()
+        copy(RF + n, relay.at[n], relay.at[n], {"ctx": sib}).wait_send()
+    for n in range(5):
+        copy(PD + n, psend.at[0], precv.at[dp], {"ctx": sib}).wait_send()
 
 
 def local(
@@ -278,7 +308,7 @@
         in_specs=[vm] * 10 + [sm] * 2,
         out_specs=vm,
         scratch_shapes=[
-            pltpu.VMEM((16, 2, 144, 256), BF16),
+            pltpu.VMEM((16, 4, 144, 128), BF16),
             pltpu.VMEM((4, 144, 256), BF16),
             pltpu.VMEM((2, 16, 2, 64, 256), BF16),
             pltpu.VMEM((256, 512), F32),
@@ -289,6 +319,7 @@
             pltpu.VMEM((4, 8, 128), F32),
             pltpu.VMEM((8, 128, 512), BF16),
             pltpu.VMEM((8, 128, 512), BF16),
+            pltpu.VMEM((4, 64, 512), BF16),
             pltpu.VMEM((8, 128), F32),
             pltpu.VMEM((8, 8, 128), F32),
             pltpu.VMEM((128, 256), BF16),

time: 85.7 us -> 84.8 us (0.989)
  no operation moved by 1% of the time
where the time goes in v3:
time: 84.8 us; the launch traced here: 84.7 us
  Pallas kernels  81.8 us (96%)
  local copies, waits for them, and re-layouts  2.16 us (3%)
    pallas_call x1, Pallas kernels, local(): pl.pallas_call(kernel, out_shape=jax.ShapeDtypeStruct(residual.shape, BF1...  81.8 us

profile of v3, /device:TPU:1, one launch (start us, length us, event | category | flops | bytes accessed | tf_op | source)
XLA Modules:
  0.0 84.7 jit_solution(6471384295617977779)
XLA Ops:
  0.0 0.0 copy-start
  0.7 0.0 copy-done
  0.7 0.6 reshape.3.gain_in
  1.3 81.8 %shard_map.118 = bf16[128,512]{1,0:T(8,128)(2,1)} custom-call(bf16[128,256]{1,0:T(8,128)(2,1)} %q_in.1, bf16[128,256]{1,0:T(8,128)(2,1)} %k_in.1, bf16[128,256]{1,0:T(8,128)(2,1)} %v_in.1, bf16[32,256]{1,0:T(8,128)(2,1)} %ok_in.1, bf16[32,256]{1,0:T(8,128)(2,1)} %ov_in.1, bf16[2,4,128,128]{3,2,1,0:T(8,128)(2,1)} %ck_in.1, bf16[2,4,128,128]{3,2,1,0:T(8,128)(2,1)} %cv_in.1, ...), custom_call_target="tpu_custom_call" | custom-call | tf_op jit(solution)/shard_map/pallas_call | solution.py:305
  83.1 1.6 %copy.15 = bf16[128,512]{1,0:T(8,128)(2,1)} copy(bf16[128,512]{1,0:T(8,128)(2,1)} %shard_map.118) | data formatting | bytes 262144
Async XLA Ops:
  0.0 0.7 copy-start

commit v4 on v3

--- a/solution.py
+++ b/solution.py
@@ -104,13 +104,6 @@
     for c in (2, 3):
         same(KU + c * 8, kv.at[z, c], up).start()
         same(KD + c * 8, kv.at[z, c], down).start()
-    same(WY, wall.at[1 - y, z, core], other).wait_recv()
-    same(WU, w_of(z, core), up).start()
-    same(WD, w_of(z, core), down).start()
-    same(SX, w_of(z, core), sib).start()
-    for k, (fy, fc) in enumerate(((1 - y, core), (1 - y, 1 - core), (y, 1 - core))):
-        same(QQ + k, qb.at[fy * 2 + fc], other).wait_recv()
-
     factor = math.log2(math.e) / math.sqrt(128.0)
     r = lax.broadcasted_iota(jnp.int32, (144, 128), 0)
     rf = r.astype(F32)
@@ -149,28 +142,41 @@
             rows[h + 2 : h + 3, :] = rows[h + 2 : h + 3, :] * shrink + jnp.sum(p, axis=0, keepdims=True)
             acc[cols, :] = acc[cols, :] * shrink + dot(vals, p.astype(BF16), 0, 0)
 
-    fold([z])
-
-    def stage(s, carry):
-        lo, hi = behind(s), ahead(s)
+    def ring(s):
         for c in range(4):
-            for base, at_z, to in ((KU + c * 8, lo, up), (KD + c * 8, hi, down)):
+            for base, at_z, to in ((KU + c * 8, behind(s), up), (KD + c * 8, ahead(s), down)):
                 same(base + s - 1, kv.at[at_z, c], to).wait_recv()
                 same(base + s, kv.at[at_z, c], to).start()
-        fold([lo, hi])
-        for base, side, at_z, to in ((WU, SU, lo, up), (WD, SD, hi, down)):
+
+    def ring_w(s):
+        for base, side, at_z, to in ((WU, SU, behind(s), up), (WD, SD, ahead(s), down)):
             same(base + s - 1, w_of(at_z, core), to).wait_recv()
             same(base + s, w_of(at_z, core), to).start()
             same(side + s - 1, w_of(at_z, core), sib).start()
+
+    ring(1)
+    same(WY, wall.at[1 - y, z, core], other).wait_recv()
+    same(WU, w_of(z, core), up).start()
+    same(WD, w_of(z, core), down).start()
+    same(SX, w_of(z, core), sib).start()
+    for k, (fy, fc) in enumerate(((1 - y, core), (1 - y, 1 - core), (y, 1 - core))):
+        same(QQ + k, qb.at[fy * 2 + fc], other).wait_recv()
+
+    def stage(s, carry):
+        fold([behind(s), ahead(s)])
+        ring(s + 1)
+        ring_w(s)
         return carry
 
-    lax.fori_loop(1, 7, stage, 0)
+    lax.fori_loop(1, 6, stage, 0)
+    fold([behind(6), ahead(6)])
     lo, hi, far = behind(7), ahead(7), ahead(8)
     for c in range(4):
         for base, at_z, to in ((KU + c * 8, lo, up), (KD + c * 8, hi, down)):
             same(base + 6, kv.at[at_z, c], to).wait_recv()
             if (to is up) == (c % 2 == 0):
                 same(base + 7, kv.at[at_z, c], to).start()
+    ring_w(6)
     fold([lo, hi])
     for base, side, at_z, to, fy in ((WU, SU, lo, up, 0), (WD, SD, hi, down, 1)):
         same(base + 6, w_of(at_z, core), to).wait_recv()
@@ -178,7 +184,7 @@
         same(side + 6, w_of(at_z, core), sib).start()
     for c in range(4):
         same((KD if c % 2 else KU) + c * 8 + 7, kv.at[far, c], up).wait_recv()
-    fold([far])
+    fold([far, z])
 
     for k, (fy, fc) in enumerate(((1 - y, core), (1 - y, 1 - core), (y, 1 - core))):
         m = fy * 2 + fc
@@ -265,10 +271,9 @@
         copy(PW + k - 1, pwsend, pwrecv.at[src], {"dp": src}).wait_recv()
     power = jnp.sum(pwrecv[...], axis=0)[0:1] / 4096.0
     norm = jnp.broadcast_to(lax.rsqrt(power + 1e-6), (128, 128)).T
-    gain = gain_in[...].astype(F32)
     for c in range(4):
         cols = slice(c * 128, (c + 1) * 128)
-        out_ref[:, cols] = (stream_s[:, cols] * norm * gain[:, cols]).astype(BF16)
+        out_ref[:, cols] = (stream_s[:, cols] * norm * gain_in[cols].astype(F32).reshape(1, 128)).astype(BF16)
 
     for s in range(8):
         for c in range(4):
@@ -330,7 +335,7 @@
         compiler_params=pltpu.CompilerParams(collective_id=0, has_side_effects=True),
     )(
         queries, keys, values, old_keys, old_values, conv_keys, conv_values, out_proj, residual,
-        gain.reshape(1, -1), span_order, memory_length,
+        gain, span_order, memory_length,
     )
 
 

time: 84.8 us -> 83.1 us (0.980)
  Pallas kernels: 81.8 us -> 80.8 us
    pallas_call x1, Pallas kernels: 81.8 us -> 80.8 us  [local(): pl.pallas_call(kernel, out_shape=jax.ShapeDtypeStruct(residual.shape, BF1...]
where the time goes in v4:
time: 83.1 us; the launch traced here: 83 us
  Pallas kernels  80.8 us (97%)
  local copies, waits for them, and re-layouts  1.57 us (2%)
    pallas_call x1, Pallas kernels, local(): pl.pallas_call(kernel, out_shape=jax.ShapeDtypeStruct(residual.shape, BF1...  80.8 us

profile of v4, /device:TPU:1, one launch (start us, length us, event | category | flops | bytes accessed | tf_op | source)
XLA Modules:
  0.0 83.0 jit_solution(3968079346238547496)
XLA Ops:
  0.7 80.8 %shard_map.118 = bf16[128,512]{1,0:T(8,128)(2,1)} custom-call(bf16[128,256]{1,0:T(8,128)(2,1)} %q_in.1, bf16[128,256]{1,0:T(8,128)(2,1)} %k_in.1, bf16[128,256]{1,0:T(8,128)(2,1)} %v_in.1, bf16[32,256]{1,0:T(8,128)(2,1)} %ok_in.1, bf16[32,256]{1,0:T(8,128)(2,1)} %ov_in.1, bf16[2,4,128,128]{3,2,1,0:T(8,128)(2,1)} %ck_in.1, bf16[2,4,128,128]{3,2,1,0:T(8,128)(2,1)} %cv_in.1, ...), custom_call_target="tpu_custom_call" | custom-call | tf_op jit(solution)/shard_map/pallas_call | solution.py:310
  81.4 1.6 %copy.15 = bf16[128,512]{1,0:T(8,128)(2,1)} copy(bf16[128,512]{1,0:T(8,128)(2,1)} %shard_map.118) | data formatting | bytes 262144

commit v5 on v4

--- a/solution.py
+++ b/solution.py
@@ -182,9 +182,10 @@
         same(base + 6, w_of(at_z, core), to).wait_recv()
         same(base + 7, wall.at[fy, at_z, core], to).start()
         same(side + 6, w_of(at_z, core), sib).start()
+    fold([z])
     for c in range(4):
         same((KD if c % 2 else KU) + c * 8 + 7, kv.at[far, c], up).wait_recv()
-    fold([far, z])
+    fold([far])
 
     for k, (fy, fc) in enumerate(((1 - y, core), (1 - y, 1 - core), (y, 1 - core))):
         m = fy * 2 + fc

time: 83.1 us -> 83.6 us (level)
  no operation moved by 1% of the time
where the time goes in v5:
time: 83.6 us; the launch traced here: 83.4 us
  Pallas kernels  81.2 us (97%)
  local copies, waits for them, and re-layouts  1.57 us (2%)
    pallas_call x1, Pallas kernels, local(): pl.pallas_call(kernel, out_shape=jax.ShapeDtypeStruct(residual.shape, BF1...  81.2 us

profile of v5, /device:TPU:1, one launch (start us, length us, event | category | flops | bytes accessed | tf_op | source)
XLA Modules:
  0.0 83.4 jit_solution(15658800136231026965)
XLA Ops:
  0.7 81.2 %shard_map.118 = bf16[128,512]{1,0:T(8,128)(2,1)} custom-call(bf16[128,256]{1,0:T(8,128)(2,1)} %q_in.1, bf16[128,256]{1,0:T(8,128)(2,1)} %k_in.1, bf16[128,256]{1,0:T(8,128)(2,1)} %v_in.1, bf16[32,256]{1,0:T(8,128)(2,1)} %ok_in.1, bf16[32,256]{1,0:T(8,128)(2,1)} %ov_in.1, bf16[2,4,128,128]{3,2,1,0:T(8,128)(2,1)} %ck_in.1, bf16[2,4,128,128]{3,2,1,0:T(8,128)(2,1)} %cv_in.1, ...), custom_call_target="tpu_custom_call" | custom-call | tf_op jit(solution)/shard_map/pallas_call | solution.py:311
  81.9 1.6 %copy.15 = bf16[128,512]{1,0:T(8,128)(2,1)} copy(bf16[128,512]{1,0:T(8,128)(2,1)} %shard_map.118) | data formatting | bytes 262144
